TPU v7x, 256 devices: a whole 4x4x8 slice. The times are simulated.
256 devices in a mesh: chan: 8 (over x, core), ctx: 32 (over z, y).
Axes of the slice: x: 4, y: 4, z: 8, core: 2. Of those that a mesh axis runs over, the one named last changes fastest.
Arguments:
- queries: bfloat16 [4096, 8192], P('ctx', 'chan'), may hold values from -6 to 6
- keys: bfloat16 [4096, 8192], P('ctx', 'chan'), may hold values from -6 to 6
- values: bfloat16 [4096, 8192], P('ctx', 'chan'), may hold values from -6 to 6
- filters: bfloat16 [4, 4096], P(None, 'ctx'), may hold values from -0.09375 to 0.09375
- cotangent: bfloat16 [4096, 8192], P('ctx', 'chan'), may hold values from -6 to 6
Outputs:
- output: bfloat16 [4096, 8192], P('ctx', 'chan')
- query_grad: bfloat16 [4096, 8192], P('ctx', 'chan')
- key_grad: bfloat16 [4096, 8192], P('ctx', 'chan')
- value_grad: bfloat16 [4096, 8192], P('ctx', 'chan')
- filter_grad: float32 [4, 4096], P(None, 'ctx')
All inputs are finite; a program needn't handle non-finite values.
Results may differ from a plain program's by a relative error of at most 0.015.
Values may be sent and summed in bfloat16 or wider, within the bound.
A program may use at most 64 MiB of HBM per device.

v0:
```python
import jax
import jax.numpy as jnp
from jax import lax
from jax.sharding import PartitionSpec as P

D = 8192
NFILT = 4


def toeplitz(padded, base, height, breadth):
    middle = padded.shape[1] // 2
    span = height + breadth - 1
    window = lax.dynamic_slice_in_dim(padded, middle + base - breadth + 1, span, 1)
    flipped = window[:, ::-1]
    tiled = jnp.tile(flipped, (1, height + 1))
    flat = tiled[:, height - 1 : height - 1 + height * (span - 1)]
    return flat.reshape(padded.shape[0], height, span - 1)[:, :, :breadth]


def diagonal_sums(product):
    nfil, height, breadth = product.shape
    stride = height + breadth
    flipped = product[:, :, ::-1]
    padded = jnp.pad(flipped, ((0, 0), (0, 0), (0, height)))
    flat = padded.reshape(nfil, height * stride)[:, : height * (stride - 1)]
    return jnp.sum(flat.reshape(nfil, height, stride - 1), axis=1)


def add_lags(lag_acc, sums, first_lag):
    middle = lag_acc.shape[1] // 2
    where = middle + first_lag
    current = lax.dynamic_slice_in_dim(lag_acc, where, sums.shape[1], 1)
    return lax.dynamic_update_slice_in_dim(lag_acc, current + sums, where, 1)


def in_blocks(block_fn, carry, piece, rows):
    count = piece.shape[0]
    size = rows * max(1, 512 // rows)
    parts = piece.reshape((count // size, size) + piece.shape[1:])
    offsets = jnp.arange(count // size, dtype=jnp.int32) * size

    def visit(state, item):
        block, offset = item
        return (block_fn(state, block, offset), None)

    result, unused = lax.scan(visit, carry, (parts, offsets))
    return result


def shards(queries, keys, values, filters, cotangent):
    rows, width = queries.shape
    nfil = filters.shape[0]
    narrow = width // nfil
    gated = (keys.astype(jnp.float32) * values.astype(jnp.float32)).astype(jnp.bfloat16)
    back = (cotangent.astype(jnp.float32) * queries.astype(jnp.float32)).astype(jnp.bfloat16)
    taps = lax.all_gather(filters, "ctx", axis=1, tiled=True)
    total = taps.shape[1]
    padded = jnp.concatenate([jnp.zeros_like(taps), taps], axis=1)
    lag_start = jnp.zeros((nfil, 2 * total), jnp.float32)
    first = lax.axis_index("ctx") * rows
    back_cols = back.reshape(rows, narrow, nfil)

    def forward_block(carry, piece, start):
        count = piece.shape[0]

        def forward_work(state):
            mixed_acc, lag_acc = state
            tile = toeplitz(padded, first - start, rows, count)
            columns = piece.reshape(count, narrow, nfil)
            mixed_acc = mixed_acc + jnp.einsum(
                "fst,tcf->scf", tile, columns, preferred_element_type=jnp.float32
            )
            product = jnp.einsum(
                "scf,tcf->fst", back_cols, columns, preferred_element_type=jnp.float32
            )
            lag_acc = add_lags(lag_acc, diagonal_sums(product), first - start - count + 1)
            return (mixed_acc, lag_acc)

        return lax.cond(start < first + rows, forward_work, lambda state: state, carry)

    empty = jnp.zeros((rows, narrow, nfil), jnp.float32)
    mixed_acc, lag_part = in_blocks(
        forward_block, (empty, lag_start), lax.all_gather(gated, "ctx", axis=0, tiled=True), rows
    )

    def backward_block(grad_acc, piece, start):
        count = piece.shape[0]

        def backward_work(state):
            tile = toeplitz(padded, start - first, count, rows)
            columns = piece.reshape(count, narrow, nfil)
            return state + jnp.einsum(
                "fst,scf->tcf", tile, columns, preferred_element_type=jnp.float32
            )

        return lax.cond(start + count > first, backward_work, lambda state: state, grad_acc)

    grad_acc = in_blocks(
        backward_block, empty, lax.all_gather(back, "ctx", axis=0, tiled=True), rows
    )
    mixed = mixed_acc.reshape(rows, width)
    gated_grad = grad_acc.reshape(rows, width)
    lag_share = lax.psum_scatter(
        lag_part[:, total:].astype(jnp.bfloat16), "ctx", scatter_dimension=1, tiled=True
    ).astype(jnp.float32)
    lag_total = lax.psum(lag_share, "chan")
    scale = (total * (D // NFILT)) ** (-0.5)
    filter_grad = lag_total * scale
    output = (queries.astype(jnp.float32) * mixed).astype(jnp.bfloat16)
    query_grad = (cotangent.astype(jnp.float32) * mixed).astype(jnp.bfloat16)
    key_grad = (gated_grad * values.astype(jnp.float32)).astype(jnp.bfloat16)
    value_grad = (gated_grad * keys.astype(jnp.float32)).astype(jnp.bfloat16)
    return (output, query_grad, key_grad, value_grad, filter_grad)


def solution(mesh):
    placed = (
        P("ctx", "chan"),
        P("ctx", "chan"),
        P("ctx", "chan"),
        P(None, "ctx"),
        P("ctx", "chan"),
    )
    return jax.shard_map(
        shards,
        mesh=mesh,
        in_specs=placed,
        out_specs=(
            P("ctx", "chan"),
            P("ctx", "chan"),
            P("ctx", "chan"),
            P("ctx", "chan"),
            P(None, "ctx"),
        ),
        check_vma=False,
    )
```

profile of v0, /device:TPU:1, one launch (start us, length us, event | category | flops | bytes accessed | tf_op | source)
XLA Modules:
  0.0 846.8 jit_solution(6806432111096197766)
XLA Ops:
  12.5 38.3 %all_gather.9 = bf16[4,4096]{1,0:T(4,128)(2,1)S(1)} all-gather(bf16[4,128]{1,0:T(4,128)(2,1)S(1)} %copy-done.7), channel_id=1, replica_groups=mesh['chan'=8,'ctx'=32] {'ctx'}, dimensions={1}, use_global_device_ids=true | all-gather | bytes 33792 | tf_op jit(solution)/shard_map/all_gather | solution.py:56
  50.8 65.4 %all-gather.5.cloned.1.call-done = bf16[4096,1024]{0,1:T(8,128)(2,1)} async-done(((bf16[128,1024]{0,1:T(8,128)(2,1)}), bf16[4096,1024]{0,1:T(8,128)(2,1)}) %all-gather.5.cloned.1.call-update) | async-done | bytes 8388624 | tf_op jit(solution)/shard_map/all_gather | solution.py:99
  116.2 7.4 copy.60
  123.7 238.9 %while.27 = (s32[]{:T(128)}, f32[128,256,4]{1,0,2:T(8,128)S(1)}, s32[8]{0:T(128)S(1)}, s32[]{:T(128)}, bf16[4,8192]{1,0:T(4,128)(2,1)S(1)}, /*index=5*/bf16[8,512,1024]{1,2,0:T(8,128)(2,1)}, s32[]{:T(128)}, s32[]{:T(128)}) while((s32[]{:T(128)}, f32[128,256,4]{1,0,2:T(8,128)S(1)}, s32[8]{0:T(128)S(1)}, s32[]{:T(128)}, ...), condition=%wide.region_8.9_spmd, body=%wide.region_5.8_spmd.sunk | while | flops 134348800 | bytes 35643552 | solution.py:46
  125.0 28.5 %conditional.5 = (f32[128,256,4]{1,0,2:T(8,128)S(1)}) conditional(s32[]{:T(128)} %convert_element_type.91, f32[128,256,4]{1,0,2:T(8,128)S(1)} %get-tuple-element.399, (s32[]{:T(128)}, s32[]{:T(128)}, bf16[4,8192]{1,0:T(4,128)(2,1)S(1)}, bf16[8,512,1024]{1,2,0:T(8,128)(2,1)}, s32[]{:T(128)}, /*index=5*/f32[128,256,4]{1,0,2:T(8,128)S(1)}) %tuple.73), branch_computations={%region_6.6_spmd, %region_7.7_spmd} | conditional | flops 134348800 | bytes 35643384 | solution.py:96
  126.6 6.1 reshape.68
  132.7 5.1 tile.14
  137.8 3.0 slice.28
  143.5 6.8 reshape.54
  154.9 28.5 %conditional.5 = (f32[128,256,4]{1,0,2:T(8,128)S(1)}) conditional(s32[]{:T(128)} %convert_element_type.91, f32[128,256,4]{1,0,2:T(8,128)S(1)} %get-tuple-element.399, (s32[]{:T(128)}, s32[]{:T(128)}, bf16[4,8192]{1,0:T(4,128)(2,1)S(1)}, bf16[8,512,1024]{1,2,0:T(8,128)(2,1)}, s32[]{:T(128)}, /*index=5*/f32[128,256,4]{1,0,2:T(8,128)S(1)}) %tuple.73), branch_computations={%region_6.6_spmd, %region_7.7_spmd} | conditional | flops 134348800 | bytes 35643384 | solution.py:96
  156.5 6.1 reshape.68
  162.6 5.1 tile.14
  167.7 3.0 slice.28
  173.4 6.8 reshape.54
  184.8 28.5 %conditional.5 = (f32[128,256,4]{1,0,2:T(8,128)S(1)}) conditional(s32[]{:T(128)} %convert_element_type.91, f32[128,256,4]{1,0,2:T(8,128)S(1)} %get-tuple-element.399, (s32[]{:T(128)}, s32[]{:T(128)}, bf16[4,8192]{1,0:T(4,128)(2,1)S(1)}, bf16[8,512,1024]{1,2,0:T(8,128)(2,1)}, s32[]{:T(128)}, /*index=5*/f32[128,256,4]{1,0,2:T(8,128)S(1)}) %tuple.73), branch_computations={%region_6.6_spmd, %region_7.7_spmd} | conditional | flops 134348800 | bytes 35643384 | solution.py:96
  186.3 6.1 reshape.68
  192.4 5.1 tile.14
  197.5 3.0 slice.28
  203.2 6.8 reshape.54
  214.6 28.5 %conditional.5 = (f32[128,256,4]{1,0,2:T(8,128)S(1)}) conditional(s32[]{:T(128)} %convert_element_type.91, f32[128,256,4]{1,0,2:T(8,128)S(1)} %get-tuple-element.399, (s32[]{:T(128)}, s32[]{:T(128)}, bf16[4,8192]{1,0:T(4,128)(2,1)S(1)}, bf16[8,512,1024]{1,2,0:T(8,128)(2,1)}, s32[]{:T(128)}, /*index=5*/f32[128,256,4]{1,0,2:T(8,128)S(1)}) %tuple.73), branch_computations={%region_6.6_spmd, %region_7.7_spmd} | conditional | flops 134348800 | bytes 35643384 | solution.py:96
  216.2 6.1 reshape.68
  222.3 5.1 tile.14
  227.4 3.0 slice.28
  233.1 6.8 reshape.54
  244.5 28.5 %conditional.5 = (f32[128,256,4]{1,0,2:T(8,128)S(1)}) conditional(s32[]{:T(128)} %convert_element_type.91, f32[128,256,4]{1,0,2:T(8,128)S(1)} %get-tuple-element.399, (s32[]{:T(128)}, s32[]{:T(128)}, bf16[4,8192]{1,0:T(4,128)(2,1)S(1)}, bf16[8,512,1024]{1,2,0:T(8,128)(2,1)}, s32[]{:T(128)}, /*index=5*/f32[128,256,4]{1,0,2:T(8,128)S(1)}) %tuple.73), branch_computations={%region_6.6_spmd, %region_7.7_spmd} | conditional | flops 134348800 | bytes 35643384 | solution.py:96
  246.1 6.1 reshape.68
  252.1 5.1 tile.14
  257.3 3.0 slice.28
  263.0 6.8 reshape.54
  274.4 28.5 %conditional.5 = (f32[128,256,4]{1,0,2:T(8,128)S(1)}) conditional(s32[]{:T(128)} %convert_element_type.91, f32[128,256,4]{1,0,2:T(8,128)S(1)} %get-tuple-element.399, (s32[]{:T(128)}, s32[]{:T(128)}, bf16[4,8192]{1,0:T(4,128)(2,1)S(1)}, bf16[8,512,1024]{1,2,0:T(8,128)(2,1)}, s32[]{:T(128)}, /*index=5*/f32[128,256,4]{1,0,2:T(8,128)S(1)}) %tuple.73), branch_computations={%region_6.6_spmd, %region_7.7_spmd} | conditional | flops 134348800 | bytes 35643384 | solution.py:96
  275.9 6.1 reshape.68
  282.0 5.1 tile.14
  292.8 6.8 reshape.54
  304.2 28.5 %conditional.5 = (f32[128,256,4]{1,0,2:T(8,128)S(1)}) conditional(s32[]{:T(128)} %convert_element_type.91, f32[128,256,4]{1,0,2:T(8,128)S(1)} %get-tuple-element.399, (s32[]{:T(128)}, s32[]{:T(128)}, bf16[4,8192]{1,0:T(4,128)(2,1)S(1)}, bf16[8,512,1024]{1,2,0:T(8,128)(2,1)}, s32[]{:T(128)}, /*index=5*/f32[128,256,4]{1,0,2:T(8,128)S(1)}) %tuple.73), branch_computations={%region_6.6_spmd, %region_7.7_spmd} | conditional | flops 134348800 | bytes 35643384 | solution.py:96
  305.8 6.1 reshape.68
  311.9 5.1 tile.14
  317.0 3.0 slice.28
  322.7 6.8 reshape.54
  334.1 28.5 %conditional.5 = (f32[128,256,4]{1,0,2:T(8,128)S(1)}) conditional(s32[]{:T(128)} %convert_element_type.91, f32[128,256,4]{1,0,2:T(8,128)S(1)} %get-tuple-element.399, (s32[]{:T(128)}, s32[]{:T(128)}, bf16[4,8192]{1,0:T(4,128)(2,1)S(1)}, bf16[8,512,1024]{1,2,0:T(8,128)(2,1)}, s32[]{:T(128)}, /*index=5*/f32[128,256,4]{1,0,2:T(8,128)S(1)}) %tuple.73), branch_computations={%region_6.6_spmd, %region_7.7_spmd} | conditional | flops 134348800 | bytes 35643384 | solution.py:96
  335.6 6.1 reshape.68
  341.7 5.1 tile.14
  352.6 6.8 reshape.54
  366.8 96.9 %all-gather.3.cloned.1.call-done = bf16[4096,1024]{0,1:T(8,128)(2,1)} async-done(((bf16[128,1024]{0,1:T(8,128)(2,1)}), bf16[4096,1024]{0,1:T(8,128)(2,1)}) %all-gather.3.cloned.1.call-update) | async-done | bytes 8388624 | tf_op jit(solution)/shard_map/all_gather | solution.py:83
  463.7 7.4 copy.61
  471.9 26.2 %while.26 = (s32[]{:T(128)}, f32[128,256,4]{1,0,2:T(8,128)}, f32[4,8192]{1,0:T(4,128)S(1)}, s32[8]{0:T(128)S(1)}, s32[]{:T(128)}, /*index=5*/s32[]{:T(128)}, bf1...) while((s32[]{:T(128)}, f32[128,256,4]{1,0,2:T(8,128)}, ...), condition=%wide.region_4.5_spmd, body=%wide.region_0.4_spmd.sunk | while | flops 268893696 | bytes 31679636 | solution.py:46
  473.2 16.0 %conditional.4 = ((f32[128,256,4]{1,0,2:T(8,128)}, f32[4,8192]{1,0:T(4,128)S(1)})) conditional(s32[]{:T(128)} %convert_element_type.90, (f32[128,256,4]{1,0,2:T(8,128)}, f32[4,8192]{1,0:T(4,128)S(1)}) %tuple.70, (s32[]{:T(128)}, s32[]{:T(128)}, bf16[4,8192]{1,0:T(4,128)(2,1)}, bf16[8,512,1024]{1,2,0:T(8,128)(2,1)}, s32[]{:T(128)}, ...), branch_computations={%region_1.1_spmd, %region_2.3_spmd} | conditional | flops 268893696 | bytes 31679430 | solution.py:79
  502.8 318.5 %reduce-scatter.4.cloned.1.call-done = bf16[128,4]{1,0:T(8,128)(2,1)} async-done(((bf16[4096,4]{1,0:T(8,128)(2,1)}), bf16[128,4]{1,0:T(8,128)(2,1)}) %reduce-scatter.4.cloned.1.call-update) | async-done | bytes 1040
  822.1 17.6 %psum.7 = f32[4,128]{1,0:T(4,128)S(1)} all-reduce(bf16[4,128]{1,0:T(4,128)(2,1)S(1)} %copy.50), channel_id=1, replica_groups=mesh['chan'=8,'ctx'=32] {'chan'}, use_global_device_ids=true, to_apply=%region_10.11 | all-reduce | flops 512 | bytes 3072 | tf_op jit(solution)/shard_map/psum | solution.py:106
  (155 shorter events, 101.2 us)
Async XLA Ops:
  7.2 4.5 copy-start.5
  7.2 5.3 copy-start.7
  7.2 109.0 %all-gather.5.cloned.1.call-start = ((), (), s32[]{:S(2)}) async-start(), calls=%async_computation.2 | async-start | bytes 8650752 | tf_op jit(solution)/shard_map/all_gather | solution.py:99
  8.4 115.2 %copy-start.1 = (bf16[128,1024]{0,1:T(8,128)(2,1)}, bf16[128,1024]{0,1:T(8,128)(2,1)S(1)}, u32[]{:S(2)}) copy-start(bf16[128,1024]{0,1:T(8,128)(2,1)S(1)} %copy.36) | copy-start | bytes 786436
  9.6 114.0 %copy-start.3 = (bf16[128,1024]{0,1:T(8,128)(2,1)}, bf16[128,1024]{0,1:T(8,128)(2,1)S(1)}, u32[]{:S(2)}) copy-start(bf16[128,1024]{0,1:T(8,128)(2,1)S(1)} %copy.39) | copy-start | bytes 786436
  10.4 453.2 %all-gather.3.cloned.1.call-start = ((), (), s32[]{:S(2)}) async-start(), calls=%async_computation.1 | async-start | bytes 8650752 | tf_op jit(solution)/shard_map/all_gather | solution.py:83
  362.6 108.5 %copy-start.6 = (bf16[4,8192]{1,0:T(4,128)(2,1)}, bf16[4,8192]{1,0:T(4,128)(2,1)S(1)}, u32[]{:S(2)}) copy-start(bf16[4,8192]{1,0:T(4,128)(2,1)S(1)} %get-tuple-element.458) | copy-start | bytes 196612
  362.6 2.3 copy-start
  364.7 456.6 %reduce-scatter.4.cloned.1.call-start = ((), (), s32[]{:S(2)}) async-start(), calls=%async_computation.3 | async-start | bytes 1081344
  498.1 2.8 copy-start.2
  498.1 2.8 copy-start.4
Sparse Core Ops, SparseCore 0:
  11.1 105.0 all-gather.4
  364.8 98.8 all-gather.2
  501.1 320.1 reduce-scatter.3
where the time goes:
time: 849 us; the launch traced here: 847 us
  waiting for transfers between devices  481 us (57%)
  local copies, waits for them, and re-layouts  259 us (31%)
  blocking collectives  56 us (7%)
  loops' own time  17.9 us (2%)
  matrix products  15.2 us (2%)
  between operations  14 us (2%)
    unnamed x4, waiting for transfers between devices  319 us
    all_gather x1, waiting for transfers between devices, shards(): lax.all_gather(gated, 'ctx', axis=0, tiled=True)  96.9 us
    cond x37, local copies, waits for them, and re-layouts  76.6 us
    all_gather x1, waiting for transfers between devices, shards(): lax.all_gather(back, 'ctx', axis=0, tiled=True)  65.4 us
    reshape x9, local copies, waits for them, and re-layouts, toeplitz(): return flat.reshape(padded.shape[0], height, span - 1)[:, :, :breadth]  56.2 us
    another operation x18, local copies, waits for them, and re-layouts, toeplitz(): tiled = jnp.tile(flipped, (1, height + 1))  43.2 us
    all_gather x1, blocking collectives, shards(): taps = lax.all_gather(filters, 'ctx', axis=1, tiled=True)  38.3 us
    slice x9, local copies, waits for them, and re-layouts, toeplitz(): flat = tiled[:, height - 1:height - 1 + height * (span - 1)]  24.4 us
  transfers between devices with their start and end apart: 3, of which 3 were waited for; matrix products, arithmetic and copies ran while one was open for 1% of the time, Pallas kernels for 0%

commit v1 on v0

--- a/solution.py
+++ b/solution.py
@@ -5,6 +5,14 @@
 
 D = 8192
 NFILT = 4
+
+
+def load_the_pieces_all(x_part):
+    devs = lax.axis_size("ctx")
+    trail = []
+    for tick in tuple(range(x_part.ndim)):
+        trail.append(devs if tick == 0 else 1)
+    return lax.all_to_all(jnp.tile(x_part, trail), "ctx", split_axis=0, concat_axis=0, tiled=True)
 
 
 def toeplitz(padded, base, height, breadth):
@@ -95,9 +103,7 @@
 
         return lax.cond(start + count > first, backward_work, lambda state: state, grad_acc)
 
-    grad_acc = in_blocks(
-        backward_block, empty, lax.all_gather(back, "ctx", axis=0, tiled=True), rows
-    )
+    grad_acc = in_blocks(backward_block, empty, load_the_pieces_all(back), rows)
     mixed = mixed_acc.reshape(rows, width)
     gated_grad = grad_acc.reshape(rows, width)
     lag_share = lax.psum_scatter(

time: 849 us -> 989 us (1.16)
  blocking collectives: 56 us -> 237 us
  waiting for transfers between devices: 481 us -> 421 us
  starting transfers between devices: 0.3 us -> 12.6 us
    all_gather x1, blocking collectives: 38.3 us -> 219 us  [shards(): taps = lax.all_gather(filters, 'ctx', axis=1, tiled=True)]
    all_gather x1 -> x0, waiting for transfers between devices: 65.4 us -> none  [shards(): lax.all_gather(back, 'ctx', axis=0, tiled=True)]
    all_to_all x0 -> x1, starting transfers between devices: none -> 12.3 us  [load_the_pieces_all(): lax.all_to_all(jnp.tile(x_part, trail), 'ctx', split_axis=0, concat_axis=...]
    while x3 -> x4, local copies, waits for them, and re-layouts: 1.72 us -> 13.2 us  [in_blocks(): result, unused = lax.scan(visit, carry, (parts, offsets))]
    unnamed x4 -> x3, waiting for transfers between devices: 319 us -> 319 us
  transfers between devices with their start and end apart: 3 -> 3, of which waited for: 3 -> 2; matrix products, arithmetic and copies ran while one was open for 1% -> 0% of each run, Pallas kernels for 0% -> 0%
where the time goes in v1:
time: 989 us; the launch traced here: 987 us
  waiting for transfers between devices  421 us (43%)
  local copies, waits for them, and re-layouts  267 us (27%)
  blocking collectives  237 us (24%)
  loops' own time  17 us (2%)
  matrix products  15.2 us (2%)
  between operations  14.3 us (1%)
  starting transfers between devices  12.6 us (1%)
    unnamed x3, waiting for transfers between devices  319 us
    all_gather x1, blocking collectives, shards(): taps = lax.all_gather(filters, 'ctx', axis=1, tiled=True)  219 us
    all_gather x1, waiting for transfers between devices, shards(): lax.all_gather(gated, 'ctx', axis=0, tiled=True)  102 us
    cond x37, local copies, waits for them, and re-layouts  76.7 us
    reshape x9, local copies, waits for them, and re-layouts, toeplitz(): return flat.reshape(padded.shape[0], height, span - 1)[:, :, :breadth]  56.3 us
    another operation x18, local copies, waits for them, and re-layouts, toeplitz(): tiled = jnp.tile(flipped, (1, height + 1))  43.2 us
    slice x9, local copies, waits for them, and re-layouts, toeplitz(): flat = tiled[:, height - 1:height - 1 + height * (span - 1)]  24.4 us
    dynamic_slice x25, local copies, waits for them, and re-layouts, in_blocks(): result, unused = lax.scan(visit, carry, (parts, offsets))  21.5 us
  transfers between devices with their start and end apart: 3, of which 2 were waited for; matrix products, arithmetic and copies ran while one was open for 0% of the time, Pallas kernels for 0%

profile of v1, /device:TPU:1, one launch (start us, length us, event | category | flops | bytes accessed | tf_op | source)
XLA Modules:
  0.0 987.0 jit_solution(17157121163048954796)
XLA Ops:
  9.8 4.3 tile.17
  14.1 12.3 %all-to-all-start = ((bf16[32,128,1024]{2,1,0:T(8,128)(2,1)}), bf16[32,128,1024]{2,1,0:T(8,128)(2,1)}, u32[]{:S(2)}, u32[]{:S(2)}) async-start(bf16[32,128,1024]{2,1,0:T(8,128)(2,1)} %tile.17), calls=%async_computation | async-start | bytes 16777216 | tf_op jit(solution)/shard_map/all_to_all | solution.py:15
  27.5 219.3 %all_gather.6 = bf16[4,4096]{1,0:T(4,128)(2,1)S(1)} all-gather(bf16[4,128]{1,0:T(4,128)(2,1)S(1)} %copy-done.9), channel_id=1, replica_groups=mesh['chan'=8,'ctx'=32] {'ctx'}, dimensions={1}, use_global_device_ids=true | all-gather | bytes 33792 | tf_op jit(solution)/shard_map/all_gather | solution.py:64
  246.8 11.5 %copy.63 = bf16[8,512,1024]{1,2,0:T(8,128)(2,1)} copy(bf16[8,512,1024]{2,1,0:T(8,128)(2,1)} %bitcast.7) | data formatting | bytes 16777216 | tf_op jit(solution)/shard_map/while | solution.py:54
  258.3 238.0 %while.27 = (s32[]{:T(128)}, f32[128,256,4]{1,0,2:T(8,128)S(1)}, s32[8]{0:T(128)S(1)}, s32[]{:T(128)}, bf16[4,8192]{1,0:T(4,128)(2,1)S(1)}, /*index=5*/bf16[8,512,1024]{1,2,0:T(8,128)(2,1)}, s32[]{:T(128)}, s32[]{:T(128)}) while((s32[]{:T(128)}, f32[128,256,4]{1,0,2:T(8,128)S(1)}, s32[8]{0:T(128)S(1)}, s32[]{:T(128)}, ...), condition=%wide.region_8.9_spmd, body=%wide.region_5.8_spmd.sunk | while | flops 134348800 | bytes 35643552 | solution.py:54
  259.7 28.4 %conditional.5 = (f32[128,256,4]{1,0,2:T(8,128)S(1)}) conditional(s32[]{:T(128)} %convert_element_type.91, f32[128,256,4]{1,0,2:T(8,128)S(1)} %get-tuple-element.413, (s32[]{:T(128)}, s32[]{:T(128)}, bf16[4,8192]{1,0:T(4,128)(2,1)S(1)}, bf16[8,512,1024]{1,2,0:T(8,128)(2,1)}, s32[]{:T(128)}, /*index=5*/f32[128,256,4]{1,0,2:T(8,128)S(1)}) %tuple.75), branch_computations={%region_6.6_spmd, %region_7.7_spmd} | conditional | flops 134348800 | bytes 35643384 | solution.py:104
  261.1 6.1 reshape.76
  267.2 5.1 tile.15
  272.4 3.0 slice.28
  278.1 6.9 reshape.62
  289.4 28.4 %conditional.5 = (f32[128,256,4]{1,0,2:T(8,128)S(1)}) conditional(s32[]{:T(128)} %convert_element_type.91, f32[128,256,4]{1,0,2:T(8,128)S(1)} %get-tuple-element.413, (s32[]{:T(128)}, s32[]{:T(128)}, bf16[4,8192]{1,0:T(4,128)(2,1)S(1)}, bf16[8,512,1024]{1,2,0:T(8,128)(2,1)}, s32[]{:T(128)}, /*index=5*/f32[128,256,4]{1,0,2:T(8,128)S(1)}) %tuple.75), branch_computations={%region_6.6_spmd, %region_7.7_spmd} | conditional | flops 134348800 | bytes 35643384 | solution.py:104
  290.9 6.1 reshape.76
  297.0 5.1 tile.15
  302.1 3.0 slice.28
  307.8 6.9 reshape.62
  319.2 28.4 %conditional.5 = (f32[128,256,4]{1,0,2:T(8,128)S(1)}) conditional(s32[]{:T(128)} %convert_element_type.91, f32[128,256,4]{1,0,2:T(8,128)S(1)} %get-tuple-element.413, (s32[]{:T(128)}, s32[]{:T(128)}, bf16[4,8192]{1,0:T(4,128)(2,1)S(1)}, bf16[8,512,1024]{1,2,0:T(8,128)(2,1)}, s32[]{:T(128)}, /*index=5*/f32[128,256,4]{1,0,2:T(8,128)S(1)}) %tuple.75), branch_computations={%region_6.6_spmd, %region_7.7_spmd} | conditional | flops 134348800 | bytes 35643384 | solution.py:104
  320.7 6.1 reshape.76
  326.8 5.1 tile.15
  331.9 3.0 slice.28
  337.6 6.9 reshape.62
  348.9 28.4 %conditional.5 = (f32[128,256,4]{1,0,2:T(8,128)S(1)}) conditional(s32[]{:T(128)} %convert_element_type.91, f32[128,256,4]{1,0,2:T(8,128)S(1)} %get-tuple-element.413, (s32[]{:T(128)}, s32[]{:T(128)}, bf16[4,8192]{1,0:T(4,128)(2,1)S(1)}, bf16[8,512,1024]{1,2,0:T(8,128)(2,1)}, s32[]{:T(128)}, /*index=5*/f32[128,256,4]{1,0,2:T(8,128)S(1)}) %tuple.75), branch_computations={%region_6.6_spmd, %region_7.7_spmd} | conditional | flops 134348800 | bytes 35643384 | solution.py:104
  350.4 6.1 reshape.76
  356.5 5.1 tile.15
  367.3 6.9 reshape.62
  378.7 28.4 %conditional.5 = (f32[128,256,4]{1,0,2:T(8,128)S(1)}) conditional(s32[]{:T(128)} %convert_element_type.91, f32[128,256,4]{1,0,2:T(8,128)S(1)} %get-tuple-element.413, (s32[]{:T(128)}, s32[]{:T(128)}, bf16[4,8192]{1,0:T(4,128)(2,1)S(1)}, bf16[8,512,1024]{1,2,0:T(8,128)(2,1)}, s32[]{:T(128)}, /*index=5*/f32[128,256,4]{1,0,2:T(8,128)S(1)}) %tuple.75), branch_computations={%region_6.6_spmd, %region_7.7_spmd} | conditional | flops 134348800 | bytes 35643384 | solution.py:104
  380.2 6.1 reshape.76
  386.3 5.1 tile.15
  391.4 3.0 slice.28
  397.1 6.9 reshape.62
  408.4 28.4 %conditional.5 = (f32[128,256,4]{1,0,2:T(8,128)S(1)}) conditional(s32[]{:T(128)} %convert_element_type.91, f32[128,256,4]{1,0,2:T(8,128)S(1)} %get-tuple-element.413, (s32[]{:T(128)}, s32[]{:T(128)}, bf16[4,8192]{1,0:T(4,128)(2,1)S(1)}, bf16[8,512,1024]{1,2,0:T(8,128)(2,1)}, s32[]{:T(128)}, /*index=5*/f32[128,256,4]{1,0,2:T(8,128)S(1)}) %tuple.75), branch_computations={%region_6.6_spmd, %region_7.7_spmd} | conditional | flops 134348800 | bytes 35643384 | solution.py:104
  409.9 6.1 reshape.76
  416.0 5.1 tile.15
  426.8 6.9 reshape.62
  438.2 28.4 %conditional.5 = (f32[128,256,4]{1,0,2:T(8,128)S(1)}) conditional(s32[]{:T(128)} %convert_element_type.91, f32[128,256,4]{1,0,2:T(8,128)S(1)} %get-tuple-element.413, (s32[]{:T(128)}, s32[]{:T(128)}, bf16[4,8192]{1,0:T(4,128)(2,1)S(1)}, bf16[8,512,1024]{1,2,0:T(8,128)(2,1)}, s32[]{:T(128)}, /*index=5*/f32[128,256,4]{1,0,2:T(8,128)S(1)}) %tuple.75), branch_computations={%region_6.6_spmd, %region_7.7_spmd} | conditional | flops 134348800 | bytes 35643384 | solution.py:104
  439.7 6.1 reshape.76
  445.8 5.1 tile.15
  456.6 6.9 reshape.62
  467.9 28.4 %conditional.5 = (f32[128,256,4]{1,0,2:T(8,128)S(1)}) conditional(s32[]{:T(128)} %convert_element_type.91, f32[128,256,4]{1,0,2:T(8,128)S(1)} %get-tuple-element.413, (s32[]{:T(128)}, s32[]{:T(128)}, bf16[4,8192]{1,0:T(4,128)(2,1)S(1)}, bf16[8,512,1024]{1,2,0:T(8,128)(2,1)}, s32[]{:T(128)}, /*index=5*/f32[128,256,4]{1,0,2:T(8,128)S(1)}) %tuple.75), branch_computations={%region_6.6_spmd, %region_7.7_spmd} | conditional | flops 134348800 | bytes 35643384 | solution.py:104
  469.4 6.1 reshape.76
  475.5 5.1 tile.15
  480.6 3.0 slice.28
  486.4 6.9 reshape.62
  500.6 102.5 %all-gather.2.cloned.1.call-done = bf16[4096,1024]{0,1:T(8,128)(2,1)} async-done(((bf16[128,1024]{0,1:T(8,128)(2,1)}), bf16[4096,1024]{0,1:T(8,128)(2,1)}) %all-gather.2.cloned.1.call-update) | async-done | bytes 8388624 | tf_op jit(solution)/shard_map/all_gather | solution.py:91
  603.1 7.4 copy.78
  611.4 26.2 %while.26 = (s32[]{:T(128)}, f32[128,256,4]{1,0,2:T(8,128)}, f32[4,8192]{1,0:T(4,128)S(1)}, s32[8]{0:T(128)S(1)}, s32[]{:T(128)}, /*index=5*/s32[]{:T(128)}, bf1...) while((s32[]{:T(128)}, f32[128,256,4]{1,0,2:T(8,128)}, ...), condition=%wide.region_4.5_spmd, body=%wide.region_0.4_spmd.sunk | while | flops 268893696 | bytes 31679636 | solution.py:54
  612.6 16.0 %conditional.4 = ((f32[128,256,4]{1,0,2:T(8,128)}, f32[4,8192]{1,0:T(4,128)S(1)})) conditional(s32[]{:T(128)} %convert_element_type.90, (f32[128,256,4]{1,0,2:T(8,128)}, f32[4,8192]{1,0:T(4,128)S(1)}) %tuple.72, (s32[]{:T(128)}, s32[]{:T(128)}, bf16[4,8192]{1,0:T(4,128)(2,1)}, bf16[8,512,1024]{1,2,0:T(8,128)(2,1)}, s32[]{:T(128)}, ...), branch_computations={%region_1.1_spmd, %region_2.3_spmd} | conditional | flops 268893696 | bytes 31679430 | solution.py:87
  642.2 318.9 %reduce-scatter.4.cloned.1.call-done = bf16[128,4]{1,0:T(8,128)(2,1)} async-done(((bf16[4096,4]{1,0:T(8,128)(2,1)}), bf16[128,4]{1,0:T(8,128)(2,1)}) %reduce-scatter.4.cloned.1.call-update) | async-done | bytes 1040
  961.9 17.6 %psum.7 = f32[4,128]{1,0:T(4,128)S(1)} all-reduce(bf16[4,128]{1,0:T(4,128)(2,1)S(1)} %copy.70), channel_id=1, replica_groups=mesh['chan'=8,'ctx'=32] {'chan'}, use_global_device_ids=true, to_apply=%region_10.11 | all-reduce | flops 512 | bytes 3072 | tf_op jit(solution)/shard_map/psum | solution.py:112
  (160 shorter events, 102.5 us)
Async XLA Ops:
  8.3 5.8 copy-start.2
  9.5 4.6 copy-start.4
  9.6 4.5 copy-start
  14.1 12.4 %copy-start.6 = (bf16[128,1024]{1,0:T(8,128)(2,1)S(1)}, bf16[128,1024]{1,0:T(8,128)(2,1)}, u32[]{:S(2)}) copy-start(bf16[128,1024]{1,0:T(8,128)(2,1)} %param.14) | copy-start | bytes 786436
  14.1 12.6 %copy-start.7 = (bf16[128,1024]{1,0:T(8,128)(2,1)S(1)}, bf16[128,1024]{1,0:T(8,128)(2,1)}, u32[]{:S(2)}) copy-start(bf16[128,1024]{1,0:T(8,128)(2,1)} %param.15) | copy-start | bytes 786436
  14.1 13.4 %copy-start.9 = (bf16[4,128]{1,0:T(4,128)(2,1)S(1)}, bf16[4,128]{1,0:T(4,128)(2,1)}, u32[]{:S(2)}) copy-start(bf16[4,128]{1,0:T(4,128)(2,1)} %param.16) | copy-start | bytes 3076
  14.1 232.7 %all-to-all-start = ((bf16[32,128,1024]{2,1,0:T(8,128)(2,1)}), bf16[32,128,1024]{2,1,0:T(8,128)(2,1)}, u32[]{:S(2)}, u32[]{:S(2)}) async-start(bf16[32,128,1024]{2,1,0:T(8,128)(2,1)} %tile.17), calls=%async_computation | async-start | bytes 16777216 | tf_op jit(solution)/shard_map/all_to_all | solution.py:15
  26.4 576.7 %all-gather.2.cloned.1.call-start = ((), (), s32[]{:S(2)}) async-start(), calls=%async_computation.2 | async-start | bytes 8650752 | tf_op jit(solution)/shard_map/all_gather | solution.py:91
  496.4 114.1 %copy-start.8 = (bf16[4,8192]{1,0:T(4,128)(2,1)}, bf16[4,8192]{1,0:T(4,128)(2,1)S(1)}, u32[]{:S(2)}) copy-start(bf16[4,8192]{1,0:T(4,128)(2,1)S(1)} %get-tuple-element.470) | copy-start | bytes 196612
  496.4 2.3 copy-start.1
  498.5 462.6 %reduce-scatter.4.cloned.1.call-start = ((), (), s32[]{:S(2)}) async-start(), calls=%async_computation.3 | async-start | bytes 1081344
  637.6 2.8 copy-start.3
  637.6 2.8 copy-start.5
Sparse Core Ops, SparseCore 0:
  498.6 104.4 all-gather.1
  640.5 320.5 reduce-scatter.3
